TPU v7x, 512 devices: a whole 4x4x16 slice. The times are simulated.
512 devices in a mesh: dp: 8 (over z_hi, core), ctx: 64 (over x, z_lo, y).
Axes of the slice: x: 4, y: 4, z: 16 (z_hi: 4, z_lo: 4; z = z_hi * 4 + z_lo), core: 2. Of those that a mesh axis runs over, the one named last changes fastest.
Arguments:
- queries: bfloat16 [8, 2048, 8192], P('dp', None, 'ctx'), may hold values from -6 to 6
- keys: bfloat16 [8, 2048, 8192], P('dp', None, 'ctx'), may hold values from -6 to 6
- values: bfloat16 [8, 2048, 8192], P('dp', None, 'ctx'), may hold values from -6 to 6
- cotangent: bfloat16 [8, 2048, 8192], P('dp', None, 'ctx'), may hold values from -6 to 6
- residues: float32 [2048, 16], P(('dp', 'ctx')), may hold values from -1.5 to 1.5
- decays: float32 [2048, 16], P(('dp', 'ctx')), may hold values from 0.1 to 800
Outputs:
- mixed: bfloat16 [8, 2048, 8192], P('dp', None, 'ctx')
- grad_queries: bfloat16 [8, 2048, 8192], P('dp', None, 'ctx')
- grad_keys: bfloat16 [8, 2048, 8192], P('dp', None, 'ctx')
- grad_values: bfloat16 [8, 2048, 8192], P('dp', None, 'ctx')
- grad_residues: float32 [2048, 16], P(('dp', 'ctx'))
All inputs are finite; a program needn't handle non-finite values.
Results may differ from a plain program's by a relative error of at most 0.0057.
Values may be sent and summed in bfloat16 or wider, within the bound.
A program may use at most 64 MiB of HBM per device.

v0:
```python
import math
import jax
import jax.numpy as jnp
from jax import lax
from jax.sharding import PartitionSpec as P

exact_mode = lax.Precision.HIGHEST


def shift_along(x, axis, n, step):
    if step > 0:
        pairs = [(i, i + step) for i in range(n - step)]
    else:
        pairs = [(i, i + step) for i in range(-step, n)]
    return lax.ppermute(x, axis, perm=pairs)


def chunk_scan(state, chunk_decay, axis, n, direction):
    carry = shift_along(state, axis, n, direction)
    hop = 1
    while hop < n:
        carry = carry + jnp.exp(-chunk_decay * hop) * shift_along(carry, axis, n, direction * hop)
        hop *= 2
    return carry


def body(queries, keys, values, cotangent, residues, decays):
    n_dp = lax.axis_size("dp")
    n_ctx = lax.axis_size("ctx")
    seq_count, channels, chunk = keys.shape
    order = residues.shape[1]
    length = chunk * n_ctx
    f32 = jnp.float32
    params = lax.all_gather(
        jnp.concatenate([residues, decays], axis=1), ("dp", "ctx"), axis=0, tiled=True
    )
    dec = params[:, order:]
    scale = jnp.sqrt(1.0 - jnp.exp(-2.0 * dec / length))
    weight = params[:, :order] * scale
    gated_in = (keys.astype(f32) * values.astype(f32)).astype(jnp.bfloat16)
    gated_grad = (cotangent.astype(f32) * queries.astype(f32)).astype(jnp.bfloat16)
    g = gated_in[0].astype(f32)
    gg = gated_grad[0].astype(f32)
    pos = jnp.arange(chunk, dtype=f32)
    mid = chunk // 2
    dk = dec[:, :, None]
    grow = jnp.exp(dk * ((pos - mid) / length))
    shrink = jnp.exp(-dk * ((pos - mid) / length))
    upper = (pos[:, None] <= pos[None, :]).astype(f32)
    lower = (pos[:, None] >= pos[None, :]).astype(f32)
    end_fwd = jnp.sum(g[:, None, :] * jnp.exp(-dk * ((chunk - 1 - pos) / length)), axis=-1)
    start_bwd = jnp.sum(gg[:, None, :] * jnp.exp(-dk * (pos / length)), axis=-1)
    chunk_decay = dec * (chunk / length)
    carry_fwd = chunk_scan(end_fwd, chunk_decay, "ctx", n_ctx, 1)
    carry_bwd = chunk_scan(start_bwd, chunk_decay, "ctx", n_ctx, -1)
    fwd_state = shrink * jnp.einsum(
        "dnc,ct->dnt", g[:, None, :] * grow, upper, precision=exact_mode
    )
    bwd_state = grow * jnp.einsum(
        "dnc,ct->dnt", gg[:, None, :] * shrink, lower, precision=exact_mode
    )
    conv_intra = jnp.sum(weight[:, :, None] * fwd_state, axis=1)
    back_intra = jnp.sum(weight[:, :, None] * bwd_state, axis=1)
    cross_intra = jnp.sum(gg[:, None, :] * fwd_state, axis=-1)
    lead_fwd = jnp.exp(-dk * ((pos + 1) / length))
    lead_bwd = jnp.exp(-dk * ((chunk - pos) / length))
    conv_full = conv_intra + jnp.sum((weight * carry_fwd)[:, :, None] * lead_fwd, axis=1)
    back_full = back_intra + jnp.sum((weight * carry_bwd)[:, :, None] * lead_bwd, axis=1)
    cross = cross_intra + carry_fwd * jnp.sum(gg[:, None, :] * lead_fwd, axis=-1)
    total = lax.psum_scatter(cross, ("dp", "ctx"), scatter_dimension=0, tiled=True)
    own_scale = jnp.sqrt(1.0 - jnp.exp(-2.0 * decays / length))
    grad_residues = total * own_scale / math.sqrt(seq_count * n_dp * length)
    conv_f = conv_full.astype(jnp.bfloat16).astype(f32)[None]
    back_f = back_full.astype(jnp.bfloat16).astype(f32)[None]
    mixed = (queries.astype(f32) * conv_f).astype(jnp.bfloat16)
    grad_queries = (cotangent.astype(f32) * conv_f).astype(jnp.bfloat16)
    grad_keys = (back_f * values.astype(f32)).astype(jnp.bfloat16)
    grad_values = (back_f * keys.astype(f32)).astype(jnp.bfloat16)
    return (mixed, grad_queries, grad_keys, grad_values, grad_residues)


def solution(mesh):
    return jax.shard_map(
        body,
        mesh=mesh,
        in_specs=(
            P("dp", None, "ctx"),
            P("dp", None, "ctx"),
            P("dp", None, "ctx"),
            P("dp", None, "ctx"),
            P(("dp", "ctx"), None),
            P(("dp", "ctx"), None),
        ),
        out_specs=(
            P("dp", None, "ctx"),
            P("dp", None, "ctx"),
            P("dp", None, "ctx"),
            P("dp", None, "ctx"),
            P(("dp", "ctx"), None),
        ),
        check_vma=False,
    )
```

profile of v0, /device:TPU:1, one launch (start us, length us, event | category | flops | bytes accessed | tf_op | source)
XLA Modules:
  0.0 1972.8 jit_solution(14904116960434394480)
XLA Ops:
  8.0 1328.5 %all-gather = f32[512,4,32]{2,1,0:T(4,128)S(1)} all-gather(f32[1,4,32]{2,1,0:T(4,128)S(1)} %maximum_bitcast_fusion), channel_id=1, replica_groups=mesh['dp'=8,'ctx'=64] {'dp','ctx'}, dimensions={0}, use_global_device_ids=true | all-gather | bytes 262656 | tf_op jit(solution)/shard_map/all_gather | solution.py:34
  1338.6 3.0 multiply_reduce_fusion.6
  1343.0 1.9 collective-permute-done
  1344.9 3.8 collective-permute-start.1
  1348.7 1.9 collective-permute-done.1
  1350.7 4.1 collective-permute-start.2
  1354.8 1.9 collective-permute-done.2
  1356.8 3.5 collective-permute-start.3
  1360.3 1.9 collective-permute-done.3
  1362.2 3.5 collective-permute-start.4
  1367.7 3.5 collective-permute-start.5
  1373.2 4.3 collective-permute-start.6
  1379.2 1.7 fusion.30
  1380.9 27.1 %multiply_reduce_fusion = (f32[2048,16]{0,1:T(8,128)S(1)}, f32[2048,16]{0,1:T(8,128)S(1)}, f32[2048,128]{0,1:T(8,128)}, f32[2048,16]{0,1:T(8,128)S(1)}, f32[2048,128]{0,1:T(8,128)}) fusion(f32[2048,128]{0,1:T(8,128)} %fusion.22, f32[128]{0:T(128)S(1)} %get-tuple-element.33, f32[2048,16]{0,1:T(8,128)} %copy-done.9, f32[128]{0:T(128)S(1)} %get-tuple-element.32, ...), kind=kOutput, calls=%fused_computation | convolution fusion | flops 6508953600 | bytes 5113344 | tf_op jit(solution)/shard_map/dnc,ct->dnt/dot_general | solution.py:56
  1409.5 4.4 collective-permute-done.7
  1415.2 4.4 collective-permute-done.8
  1419.6 1.6 multiply_add_fusion
  1422.5 6.2 collective-permute-done.9
  1431.1 17.7 multiply_reduce_fusion.4
  1450.4 5.1 collective-permute-done.11
  1460.3 3.4 collective-permute-done.12
  1463.8 1.5 collective-permute-start.13
  1465.3 493.2 %all-reduce.3.cloned.1.call-done = f32[2048,16]{1,0:T(8,128)} async-done(((f32[2048,16]{1,0:T(8,128)}), f32[2048,16]{1,0:T(8,128)}) %all-reduce.3.cloned.1.call-update) | async-done | bytes 131088
  1960.8 2.8 multiply_reduce_fusion.2
  (73 shorter events, 27.4 us)
Async XLA Ops:
  7.2 1951.4 %all-reduce.3.cloned.1.call-start = ((), (), s32[]{:S(2)}) async-start(), calls=%async_computation | async-start | bytes 2097152
  1338.6 3.0 copy-start.3
  1341.6 24.2 %copy-start.7 = (bf16[1,2048,128]{2,1,0:T(8,128)(2,1)S(1)}, bf16[1,2048,128]{2,1,0:T(8,128)(2,1)}, u32[]{:S(2)}) copy-start(bf16[1,2048,128]{2,1,0:T(8,128)(2,1)} %param.9) | copy-start | bytes 1572868
  1341.6 3.4 collective-permute-start
  1344.9 5.7 collective-permute-start.1
  1350.7 6.0 collective-permute-start.2
  1356.8 5.4 collective-permute-start.3
  1362.2 5.4 collective-permute-start.4
  1367.7 5.4 collective-permute-start.5
  1373.2 6.0 collective-permute-start.6
  1379.2 28.8 %copy-start.8 = (f32[2048,16]{0,1:T(8,128)}, f32[2048,16]{0,1:T(8,128)S(1)}, u32[]{:S(2)}) copy-start(f32[2048,16]{0,1:T(8,128)S(1)} %collective-permute-done.6) | copy-start | bytes 393220
  1408.1 23.0 %copy-start.4 = (f32[2048,128]{0,1:T(8,128)S(1)}, f32[2048,128]{0,1:T(8,128)}, u32[]{:S(2)}) copy-start(f32[2048,128]{0,1:T(8,128)} %fusion.22) | copy-start | bytes 3145732
  1408.1 5.8 collective-permute-start.7
  1413.9 5.7 collective-permute-start.8
  1421.2 7.5 collective-permute-start.9
  1429.8 19.0 collective-permute-start.10
  1431.1 19.0 copy-start.1
  1431.1 19.0 copy-start.2
  1448.8 6.6 collective-permute-start.11
  1455.5 8.3 collective-permute-start.12
  1460.3 498.3 %copy-start.11 = (f32[4,16]{1,0:T(4,128)S(1)}, f32[4,16]{1,0:T(4,128)}, u32[]{:S(2)}) copy-start(f32[4,16]{1,0:T(4,128)} %param.11) | copy-start | bytes 772
  1460.3 500.5 %copy-start.10 = (f32[2048,16]{0,1:T(8,128)S(1)}, f32[2048,16]{0,1:T(8,128)}, u32[]{:S(2)}) copy-start(f32[2048,16]{0,1:T(8,128)} %copy-done.9) | copy-start | bytes 393220
  1463.8 496.0 %collective-permute-start.13 = (f32[2048,16]{0,1:T(8,128)S(1)}, f32[2048,16]{0,1:T(8,128)S(1)}, u32[]{:S(2)}, u32[]{:S(2)}) collective-permute-start(f32[2048,16]{0,1:T(8,128)S(1)} %multiply_add_fusion.1), channel_id=1, source_target_pairs={{32,0},{33,1},{34,2},{35,3},{36,4},{37,5},{38,6},{39,7},{40,8},{41... | collective-permute-start | bytes 393224 | tf_op jit(solution)/shard_map/ppermute | solution.py:15
  1960.8 2.8 copy-start
  (3 other events, 2.8 us)
Sparse Core Ops, SparseCore 0:
  1460.4 498.0 all-reduce.2
where the time goes:
time: 1970 us
  blocking collectives  1330 us (68%)
  waiting for transfers between devices  526 us (27%)
  matrix products  44.8 us (2%)
  starting transfers between devices  33.5 us (2%)
    all_gather x1, blocking collectives, body(): lax.all_gather(jnp.concatenate([residues, decays], axis=1), ('dp', 'ctx')...  1330 us
    unnamed x2, waiting for transfers between devices  493 us
  transfers between devices with their start and end apart: 15, of which 13 were waited for; matrix products, arithmetic and copies ran while one was open for 1% of the time, Pallas kernels for 0%

commit v1 on v0

--- a/solution.py
+++ b/solution.py
@@ -5,6 +5,11 @@
 from jax.sharding import PartitionSpec as P
 
 exact_mode = lax.Precision.HIGHEST
+
+
+def gather_over(x, mesh_axis, dim):
+    sent = jnp.stack([x] * lax.axis_size(mesh_axis))
+    return jnp.concatenate(lax.all_to_all(sent, mesh_axis, 0, 0), axis=dim)
 
 
 def shift_along(x, axis, n, step):
@@ -31,9 +36,7 @@
     order = residues.shape[1]
     length = chunk * n_ctx
     f32 = jnp.float32
-    params = lax.all_gather(
-        jnp.concatenate([residues, decays], axis=1), ("dp", "ctx"), axis=0, tiled=True
-    )
+    params = gather_over(jnp.concatenate([residues, decays], axis=1), ("dp", "ctx"), 0)
     dec = params[:, order:]
     scale = jnp.sqrt(1.0 - jnp.exp(-2.0 * dec / length))
     weight = params[:, :order] * scale

time: 1970 us -> 709 us (0.36)
  blocking collectives: 1330 us -> 0 us
  starting transfers between devices: 33.5 us -> 80.5 us
    all_gather x1 -> x0, blocking collectives: 1330 us -> none  [body(): lax.all_gather(jnp.concatenate([residues, decays], axis=1), ('dp', 'ctx')...]
    all_to_all x0 -> x1, starting transfers between devices: none -> 24.3 us  [gather_over(): return jnp.concatenate(lax.all_to_all(sent, mesh_axis, 0, 0), axis=dim)]
    all_to_all x0 -> x1, waiting for transfers between devices: none -> 22.8 us  [gather_over(): return jnp.concatenate(lax.all_to_all(sent, mesh_axis, 0, 0), axis=dim)]
    ppermute x14, starting transfers between devices: 33.5 us -> 56.2 us  [shift_along(): return lax.ppermute(x, axis, perm=pairs)]
  transfers between devices with their start and end apart: 15 -> 16, of which waited for: 13 -> 14; matrix products, arithmetic and copies ran while one was open for 1% -> 4% of each run, Pallas kernels for 0% -> 0%
where the time goes in v1:
time: 709 us
  waiting for transfers between devices  539 us (76%)
  starting transfers between devices  80.5 us (11%)
  matrix products  44.8 us (6%)
  other arithmetic  16.1 us (2%)
  between operations  14.5 us (2%)
  local copies, waits for them, and re-layouts  14.3 us (2%)
    unnamed x2, waiting for transfers between devices  480 us
    ppermute x14, starting transfers between devices, shift_along(): return lax.ppermute(x, axis, perm=pairs)  56.2 us
    ppermute x14, waiting for transfers between devices, shift_along(): return lax.ppermute(x, axis, perm=pairs)  35.5 us
    dot_general x1, matrix products, body(): jnp.einsum('dnc,ct->dnt', g[:, None, :] * grow, upper, precision=exact_mode)  27.1 us
    all_to_all x1, starting transfers between devices, gather_over(): return jnp.concatenate(lax.all_to_all(sent, mesh_axis, 0, 0), axis=dim)  24.3 us
    all_to_all x1, waiting for transfers between devices, gather_over(): return jnp.concatenate(lax.all_to_all(sent, mesh_axis, 0, 0), axis=dim)  22.8 us
    dot_general x1, matrix products, body(): jnp.einsum('dnc,ct->dnt', gg[:, None, :] * shrink, lower, precision=exact...  17.7 us
  transfers between devices with their start and end apart: 16, of which 14 were waited for; matrix products, arithmetic and copies ran while one was open for 4% of the time, Pallas kernels for 0%

profile of v1, /device:TPU:1, one launch (start us, length us, event | category | flops | bytes accessed | tf_op | source)
XLA Modules:
  0.0 708.7 jit_solution(12483365844610787434)
XLA Ops:
  9.5 24.3 %all-to-all-start = ((f32[512,1,128]{2,1,0:T(1,128)}), f32[512,1,128]{2,1,0:T(1,128)S(1)}, u32[]{:S(2)}, u32[]{:S(2)}) async-start(f32[512,1,128]{2,1,0:T(1,128)} %reshape.108), calls=%async_computation | async-start | bytes 524288 | tf_op jit(solution)/shard_map/all_to_all | solution.py:12
  35.4 22.8 %all-to-all-done = f32[512,1,128]{2,1,0:T(1,128)S(1)} async-done(((f32[512,1,128]{2,1,0:T(1,128)}), f32[512,1,128]{2,1,0:T(1,128)S(1)}, u32[]{:S(2)}, u32[]{:S(2)}) %all-to-all-start) | async-done | bytes 262176 | tf_op jit(solution)/shard_map/all_to_all | solution.py:12
  63.4 3.0 multiply_reduce_fusion.6
  67.8 1.9 collective-permute-done
  69.8 3.8 collective-permute-start.1
  73.5 1.9 collective-permute-done.1
  75.5 5.5 collective-permute-start.2
  81.0 1.9 collective-permute-done.2
  83.0 10.9 %collective-permute-start.3 = (f32[2048,16]{0,1:T(8,128)S(1)}, f32[2048,16]{0,1:T(8,128)S(1)}, u32[]{:S(2)}, u32[]{:S(2)}) collective-permute-start(f32[2048,16]{0,1:T(8,128)S(1)} %multiply_add_fusion.10), channel_id=1, source_target_pairs={{0,4},{1,5},{2,6},{3,7},{4,8},{5,9},{6,10},{7,11},{8,12},{9,13},{1... | collective-permute-start | bytes 393224 | tf_op jit(solution)/shard_map/ppermute | solution.py:20
  93.9 1.9 collective-permute-done.3
  95.9 3.7 collective-permute-start.4
  101.5 14.8 %collective-permute-start.5 = (f32[2048,16]{0,1:T(8,128)S(1)}, f32[2048,16]{0,1:T(8,128)S(1)}, u32[]{:S(2)}, u32[]{:S(2)}) collective-permute-start(f32[2048,16]{0,1:T(8,128)S(1)} %multiply_add_fusion.8), channel_id=1, source_target_pairs={{0,16},{1,17},{2,18},{3,19},{4,20},{5,21},{6,22},{7,23},{8,24},{9,... | collective-permute-start | bytes 393224 | tf_op jit(solution)/shard_map/ppermute | solution.py:20
  118.2 6.8 collective-permute-start.6
  126.0 2.1 collective-permute-done.6
  129.8 27.1 %multiply_reduce_fusion = (f32[2048,16]{0,1:T(8,128)S(1)}, f32[2048,16]{0,1:T(8,128)S(1)}, f32[2048,128]{0,1:T(8,128)}, f32[2048,16]{0,1:T(8,128)S(1)}, f32[2048,128]{0,1:T(8,128)}) fusion(f32[2048,128]{0,1:T(8,128)} %fusion.22, f32[128]{0:T(128)S(1)} %get-tuple-element.33, f32[2048,16]{0,1:T(8,128)} %copy-done.11, f32[128]{0:T(128)S(1)} %get-tuple-element.32, ...), kind=kOutput, calls=%fused_computation | convolution fusion | flops 6508953600 | bytes 5113344 | tf_op jit(solution)/shard_map/dnc,ct->dnt/dot_general | solution.py:59
  158.3 4.4 collective-permute-done.7
  164.0 4.4 collective-permute-done.8
  168.4 1.6 multiply_add_fusion
  171.3 6.2 collective-permute-done.9
  179.9 17.7 %multiply_reduce_fusion.4 = f32[2048,128]{0,1:T(8,128)} fusion(f32[2048,16]{0,1:T(8,128)S(1)} %copy.52, f32[128]{0:T(128)S(1)} %add_multiply_fusion.2, f32[2048,16]{0,1:T(8,128)} %copy-done.8, f32[2048,128]{0,1:T(8,128)S(1)} %copy-done.4, f32[2048,16]{0,1:T(8,128)} %copy-done.11), kind=kOutput, calls=%fused_computation.4 | convolution fusion | flops 6467371008 | bytes 2490880 | tf_op jit(solution)/shard_map/dnc,ct->dnt/dot_general | solution.py:62
  199.2 5.1 collective-permute-done.11
  209.1 4.4 collective-permute-done.12
  215.0 480.3 %all-reduce.3.cloned.1.call-done = f32[2048,16]{1,0:T(8,128)} async-done(((f32[2048,16]{1,0:T(8,128)}), f32[2048,16]{1,0:T(8,128)}) %all-reduce.3.cloned.1.call-update) | async-done | bytes 131088
  696.7 2.8 multiply_reduce_fusion.2
  (83 shorter events, 35.1 us)
Async XLA Ops:
  8.1 25.8 %copy-start.5 = (bf16[1,2048,128]{2,1,0:T(8,128)(2,1)S(1)}, bf16[1,2048,128]{2,1,0:T(8,128)(2,1)}, u32[]{:S(2)}) copy-start(bf16[1,2048,128]{2,1,0:T(8,128)(2,1)} %param.8) | copy-start | bytes 1572868
  9.5 24.6 %copy-start.6 = (bf16[1,2048,128]{2,1,0:T(8,128)(2,1)S(1)}, bf16[1,2048,128]{2,1,0:T(8,128)(2,1)}, u32[]{:S(2)}) copy-start(bf16[1,2048,128]{2,1,0:T(8,128)(2,1)} %param.7) | copy-start | bytes 1572868
  9.5 48.7 %all-to-all-start = ((f32[512,1,128]{2,1,0:T(1,128)}), f32[512,1,128]{2,1,0:T(1,128)S(1)}, u32[]{:S(2)}, u32[]{:S(2)}) async-start(f32[512,1,128]{2,1,0:T(1,128)} %reshape.108), calls=%async_computation | async-start | bytes 524288 | tf_op jit(solution)/shard_map/all_to_all | solution.py:12
  33.8 661.6 %all-reduce.3.cloned.1.call-start = ((), (), s32[]{:S(2)}) async-start(), calls=%async_computation.1 | async-start | bytes 2097152
  66.4 33.2 %copy-start.7 = (bf16[1,2048,128]{2,1,0:T(8,128)(2,1)S(1)}, bf16[1,2048,128]{2,1,0:T(8,128)(2,1)}, u32[]{:S(2)}) copy-start(bf16[1,2048,128]{2,1,0:T(8,128)(2,1)} %param.9) | copy-start | bytes 1572868
  66.4 3.4 collective-permute-start
  69.8 5.7 collective-permute-start.1
  75.5 7.5 %collective-permute-start.2 = (f32[2048,16]{0,1:T(8,128)S(1)}, f32[2048,16]{0,1:T(8,128)S(1)}, u32[]{:S(2)}, u32[]{:S(2)}) collective-permute-start(f32[2048,16]{0,1:T(8,128)S(1)} %multiply_add_fusion.11), channel_id=1, source_target_pairs={{0,2},{1,3},{2,4},{3,5},{4,6},{5,7},{6,8},{7,9},{8,10},{9,11},{10,... | collective-permute-start | bytes 393224 | tf_op jit(solution)/shard_map/ppermute | solution.py:20
  83.0 12.8 %collective-permute-start.3 = (f32[2048,16]{0,1:T(8,128)S(1)}, f32[2048,16]{0,1:T(8,128)S(1)}, u32[]{:S(2)}, u32[]{:S(2)}) collective-permute-start(f32[2048,16]{0,1:T(8,128)S(1)} %multiply_add_fusion.10), channel_id=1, source_target_pairs={{0,4},{1,5},{2,6},{3,7},{4,8},{5,9},{6,10},{7,11},{8,12},{9,13},{1... | collective-permute-start | bytes 393224 | tf_op jit(solution)/shard_map/ppermute | solution.py:20
  95.9 5.6 collective-permute-start.4
  101.5 16.7 %collective-permute-start.5 = (f32[2048,16]{0,1:T(8,128)S(1)}, f32[2048,16]{0,1:T(8,128)S(1)}, u32[]{:S(2)}, u32[]{:S(2)}) collective-permute-start(f32[2048,16]{0,1:T(8,128)S(1)} %multiply_add_fusion.8), channel_id=1, source_target_pairs={{0,16},{1,17},{2,18},{3,19},{4,20},{5,21},{6,22},{7,23},{8,24},{9,... | collective-permute-start | bytes 393224 | tf_op jit(solution)/shard_map/ppermute | solution.py:20
  118.2 9.8 %collective-permute-start.6 = (f32[2048,16]{0,1:T(8,128)S(1)}, f32[2048,16]{0,1:T(8,128)S(1)}, u32[]{:S(2)}, u32[]{:S(2)}) collective-permute-start(f32[2048,16]{0,1:T(8,128)S(1)} %multiply_add_fusion.7), channel_id=1, source_target_pairs={{0,32},{1,33},{2,34},{3,35},{4,36},{5,37},{6,38},{7,39},{8,40},{9,... | collective-permute-start | bytes 393224 | tf_op jit(solution)/shard_map/ppermute | solution.py:20
  128.1 28.8 %copy-start.10 = (f32[2048,16]{0,1:T(8,128)}, f32[2048,16]{0,1:T(8,128)S(1)}, u32[]{:S(2)}) copy-start(f32[2048,16]{0,1:T(8,128)S(1)} %collective-permute-done.6) | copy-start | bytes 393220
  156.8 23.0 %copy-start.4 = (f32[2048,128]{0,1:T(8,128)S(1)}, f32[2048,128]{0,1:T(8,128)}, u32[]{:S(2)}) copy-start(f32[2048,128]{0,1:T(8,128)} %fusion.22) | copy-start | bytes 3145732
  156.8 5.8 collective-permute-start.7
  162.7 5.7 collective-permute-start.8
  170.0 7.5 %collective-permute-start.9 = (f32[2048,16]{0,1:T(8,128)}, f32[2048,16]{0,1:T(8,128)}, u32[]{:S(2)}, u32[]{:S(2)}) collective-permute-start(f32[2048,16]{0,1:T(8,128)} %get-tuple-element.31), channel_id=1, source_target_pairs={{2,0},{3,1},{4,2},{5,3},{6,4},{7,5},{8,6},{9,7},{10,8},{11,9},{12,... | collective-permute-start | bytes 393224 | tf_op jit(solution)/shard_map/ppermute | solution.py:20
  178.5 19.0 %collective-permute-start.10 = (f32[2048,16]{0,1:T(8,128)S(1)}, f32[2048,16]{0,1:T(8,128)S(1)}, u32[]{:S(2)}, u32[]{:S(2)}) collective-permute-start(f32[2048,16]{0,1:T(8,128)S(1)} %multiply_add_fusion.4), channel_id=1, source_target_pairs={{4,0},{5,1},{6,2},{7,3},{8,4},{9,5},{10,6},{11,7},{12,8},{13,9},{1... | collective-permute-start | bytes 393224 | tf_op jit(solution)/shard_map/ppermute | solution.py:20
  197.6 6.6 collective-permute-start.11
  204.2 9.2 %collective-permute-start.12 = (f32[2048,16]{0,1:T(8,128)S(1)}, f32[2048,16]{0,1:T(8,128)S(1)}, u32[]{:S(2)}, u32[]{:S(2)}) collective-permute-start(f32[2048,16]{0,1:T(8,128)S(1)} %multiply_add_fusion.2), channel_id=1, source_target_pairs={{16,0},{17,1},{18,2},{19,3},{20,4},{21,5},{22,6},{23,7},{24,8},{25... | collective-permute-start | bytes 393224 | tf_op jit(solution)/shard_map/ppermute | solution.py:20
  209.0 486.3 %copy-start.13 = (f32[4,16]{1,0:T(4,128)S(1)}, f32[4,16]{1,0:T(4,128)}, u32[]{:S(2)}) copy-start(f32[4,16]{1,0:T(4,128)} %param.11) | copy-start | bytes 772
  209.0 487.6 %copy-start.9 = (f32[2048,16]{0,1:T(8,128)S(1)}, f32[2048,16]{0,1:T(8,128)}, u32[]{:S(2)}) copy-start(f32[2048,16]{0,1:T(8,128)} %copy-done.8) | copy-start | bytes 393220
  209.0 487.7 %copy-start.12 = (f32[2048,16]{0,1:T(8,128)S(1)}, f32[2048,16]{0,1:T(8,128)}, u32[]{:S(2)}) copy-start(f32[2048,16]{0,1:T(8,128)} %copy-done.11) | copy-start | bytes 393220
  213.5 483.1 %collective-permute-start.13 = (f32[2048,16]{0,1:T(8,128)S(1)}, f32[2048,16]{0,1:T(8,128)S(1)}, u32[]{:S(2)}, u32[]{:S(2)}) collective-permute-start(f32[2048,16]{0,1:T(8,128)S(1)} %multiply_add_fusion.1), channel_id=1, source_target_pairs={{32,0},{33,1},{34,2},{35,3},{36,4},{37,5},{38,6},{39,7},{40,8},{41... | collective-permute-start | bytes 393224 | tf_op jit(solution)/shard_map/ppermute | solution.py:20
  (6 other events, 46.2 us)
Sparse Core Ops, SparseCore 0:
  209.2 486.1 all-reduce.2
